TPU v7x, 512 devices: a whole 4x4x16 slice. The times are simulated.
512 devices in a mesh: lat: 4 (over y_hi, core), lon: 128 (over x, z, y_lo).
Axes of the slice: x: 4, y: 4 (y_hi: 2, y_lo: 2; y = y_hi * 2 + y_lo), z: 16, core: 2. Of those that a mesh axis runs over, the one named last changes fastest.
Arguments:
- features: bfloat16 [128, 1024, 1024], P('lat', 'lon'), may hold values from -18 to 18
- depth_kernel: bfloat16 [7, 7, 1024], replicated, may hold values from -0.875 to 0.875
- depth_bias: float32 [1024], replicated, may hold values from -3 to 3
- norm_gain: float32 [1024], replicated, may hold values from 0.1 to 1.9
- norm_bias: float32 [1024], replicated, may hold values from -3 to 3
- up_weight: bfloat16 [1024, 4096], P('lon', 'lat'), may hold values from -0.1875 to 0.1875
- up_bias: float32 [4096], P('lat'), may hold values from -3 to 3
- down_weight: bfloat16 [1024, 4096], P('lon', 'lat'), may hold values from -0.09375 to 0.09375
- down_bias: float32 [1024], replicated, may hold values from -3 to 3
- layer_scale: float32 [1024], replicated, may hold values from 0.3 to 2
Outputs:
- updated: bfloat16 [128, 1024, 1024], P('lat', 'lon')
All inputs are finite; a program needn't handle non-finite values.
Results may differ from a plain program's by a relative error of at most 0.0085.
Values may be sent and summed in bfloat16 or wider, within the bound.
A program may use at most 64 MiB of HBM per device.

v0:
```python
import jax
import jax.numpy as jnp
from jax import lax
from jax.sharding import PartitionSpec as P


def with_halo(block, sides, width, periodic):
    for axis, dim in sides:
        count = lax.axis_size(axis)
        forward = [(i, i + 1) for i in range(count - 1)]
        if periodic:
            forward.append((count - 1, 0))
        backward = [(target, source) for source, target in forward]
        low = lax.ppermute(
            lax.slice_in_dim(block, block.shape[dim] - width, None, axis=dim), axis, forward
        )
        high = lax.ppermute(lax.slice_in_dim(block, 0, width, axis=dim), axis, backward)
        block = jnp.concatenate([low, block, high], axis=dim)
    return block


def staged_gather(shard):
    count = lax.axis_size("lon")
    n_x, n_y = (4, 2)
    n_z = count // (n_x * n_y)
    index = lambda x, z, y: (x * n_z + z) * n_y + y
    by_y = [[index(x, z, y) for y in range(n_y)] for x in range(n_x) for z in range(n_z)]
    by_x = [[index(x, z, y) for x in range(n_x)] for z in range(n_z) for y in range(n_y)]
    by_z = [[index(x, z, y) for z in range(n_z)] for x in range(n_x) for y in range(n_y)]
    part = lax.all_gather(shard, "lon", axis=0, axis_index_groups=by_y)
    part = lax.all_gather(part, "lon", axis=0, axis_index_groups=by_x)
    part = lax.all_gather(part, "lon", axis=0, axis_index_groups=by_z)
    part = jnp.swapaxes(part, 0, 1)
    return part.reshape((count * shard.shape[0],) + shard.shape[1:])


def local(
    features,
    depth_kernel,
    depth_bias,
    norm_gain,
    norm_bias,
    up_weight,
    up_bias,
    down_weight,
    down_bias,
    layer_scale,
):
    row_count, col_count, chan_count = features.shape
    circled = with_halo(features, (("lon", 1),), 3, True)
    padded = with_halo(circled, (("lat", 0),), 3, False)
    kernel = depth_kernel.astype(jnp.float32)
    total = jnp.zeros((row_count, col_count, chan_count), jnp.float32) + depth_bias
    for row_off in range(7):
        for col_off in range(7):
            window = padded[row_off : row_off + row_count, col_off : col_off + col_count].astype(
                jnp.float32
            )
            total = total + window * kernel[row_off, col_off]
    centre = jnp.mean(total, axis=-1, keepdims=True)
    spread = jnp.mean((total - centre) ** 2, axis=-1, keepdims=True)
    normed = ((total - centre) * lax.rsqrt(spread + 1e-06) * norm_gain + norm_bias).astype(
        jnp.bfloat16
    )
    normed = normed.reshape(row_count * col_count, chan_count)
    gathered = lax.all_gather(normed, "lat", axis=0, tiled=True)
    pre = jnp.dot(gathered, staged_gather(up_weight), preferred_element_type=jnp.float32) + up_bias
    hidden = jax.nn.gelu(pre, approximate=False).astype(jnp.bfloat16)
    partial_out = lax.dot_general(
        hidden,
        staged_gather(down_weight),
        (((1,), (1,)), ((), ())),
        preferred_element_type=jnp.float32,
    )
    branch = lax.psum_scatter(
        partial_out.astype(jnp.bfloat16), "lat", scatter_dimension=0, tiled=True
    ).astype(jnp.float32)
    branch = branch.reshape(row_count, col_count, chan_count)
    updated = features.astype(jnp.float32) + layer_scale * (branch + down_bias)
    return updated.astype(jnp.bfloat16)


def solution(mesh):
    placed = (
        P("lat", "lon", None),
        P(),
        P(),
        P(),
        P(),
        P("lon", "lat"),
        P("lat"),
        P("lon", "lat"),
        P(),
        P(),
    )
    return jax.shard_map(
        local, mesh=mesh, in_specs=placed, out_specs=P("lat", "lon", None), check_vma=False
    )
```

profile of v0, /device:TPU:1, one launch (start us, length us, event | category | flops | bytes accessed | tf_op | source)
XLA Modules:
  0.0 285.6 jit_solution(13402974047549205243)
XLA Ops:
  6.5 0.0 copy-start
  6.5 0.0 copy-start.1
  6.5 0.0 all-gather.12.cloned.1.call-start
  6.5 4.3 %all-gather = bf16[16,1024]{1,0:T(8,128)(2,1)S(1)} all-gather(bf16[8,1024]{1,0:T(8,128)(2,1)} %param.15), channel_id=2, replica_groups={{0,1},{2,3},{4,5},{6,7},{8,9},{10,11},{12,13},{14,15},{16,17},{18,19},{..., dimensions={0}, use_global_device_ids=true | all-gather | bytes 49152 | tf_op jit(solution)/shard_map/all_gather | solution.py:30
  10.8 10.3 %all-gather.1 = bf16[8,8,1024]{2,1,0:T(8,128)(2,1)} all-gather(bf16[2,8,1024]{2,1,0:T(8,128)(2,1)S(1)} %bitcast.75), channel_id=3, replica_groups={{0,32,64,96},{1,33,65,97},{2,34,66,98},{3,35,67,99},{4,36,68,100},{5,37..., dimensions={0}, use_global_device_ids=true | all-gather | bytes 163840 | tf_op jit(solution)/shard_map/all_gather | solution.py:31
  21.1 0.0 all-gather.12.cloned.1.call-update
  21.2 0.0 all-gather.14.cloned.1.call-start
  21.2 1.4 fusion.79
  22.7 3.2 %collective-permute-start = (bf16[32,3,1024]{2,1,0:T(4,128)(2,1)S(1)}, bf16[32,3,1024]{2,1,0:T(4,128)(2,1)S(1)}, u32[]{:S(2)}, u32[]{:S(2)}) collective-permute-start(bf16[32,3,1024]{2,1,0:T(4,128)(2,1)S(1)} %get-tuple-element.11), channel_id=1, source_target_pairs={{0,1},{1,2},{2,3},{3,4},{4,5},{5,6},{6,7},{7,8},{8,9},{9,10},{10,1... | collective-permute-start | bytes 589832 | tf_op jit(solution)/shard_map/ppermute | solution.py:14
  25.9 12.7 %collective-permute-start.1 = (bf16[32,3,1024]{2,1,0:T(4,128)(2,1)S(1)}, bf16[32,3,1024]{2,1,0:T(4,128)(2,1)S(1)}, u32[]{:S(2)}, u32[]{:S(2)}) collective-permute-start(bf16[32,3,1024]{2,1,0:T(4,128)(2,1)S(1)} %get-tuple-element.12), channel_id=1, source_target_pairs={{1,0},{2,1},{3,2},{4,3},{5,4},{6,5},{7,6},{8,7},{9,8},{10,9},{11,1... | collective-permute-start | bytes 589832 | tf_op jit(solution)/shard_map/ppermute | solution.py:17
  38.6 4.0 %all-gather.3 = bf16[16,1024]{1,0:T(8,128)(2,1)S(1)} all-gather(bf16[8,1024]{1,0:T(8,128)(2,1)} %param.17), channel_id=5, replica_groups={{0,1},{2,3},{4,5},{6,7},{8,9},{10,11},{12,13},{14,15},{16,17},{18,19},{..., dimensions={0}, use_global_device_ids=true | all-gather | bytes 49152 | tf_op jit(solution)/shard_map/all_gather | solution.py:30
  42.6 9.8 %all-gather.4 = bf16[8,8,1024]{2,1,0:T(8,128)(2,1)} all-gather(bf16[2,8,1024]{2,1,0:T(8,128)(2,1)S(1)} %bitcast.76), channel_id=6, replica_groups={{0,32,64,96},{1,33,65,97},{2,34,66,98},{3,35,67,99},{4,36,68,100},{5,37..., dimensions={0}, use_global_device_ids=true | all-gather | bytes 163840 | tf_op jit(solution)/shard_map/all_gather | solution.py:31
  52.5 0.0 all-gather.14.cloned.1.call-update
  52.5 0.0 all-gather.10.cloned.1.call-start
  52.5 1.2 fusion.80
  53.7 0.0 copy-done
  53.7 0.0 copy-done.1
  53.8 0.1 fusion.81
  53.9 0.0 collective-permute-done
  53.9 0.0 collective-permute-done.1
  53.9 0.1 pad_maximum_fusion.4
  54.0 12.9 %collective-permute-start.2 = (bf16[3,14,1024]{2,1,0:T(8,128)(2,1)S(1)}, bf16[3,14,1024]{2,1,0:T(8,128)(2,1)S(1)}, u32[]{:S(2)}, u32[]{:S(2)}) collective-permute-start(bf16[3,14,1024]{2,1,0:T(8,128)(2,1)S(1)} %get-tuple-element.9), channel_id=1, source_target_pairs={{0,128},{128,256},{256,384},{1,129},{129,257},{257,385},{2,130},{1... | collective-permute-start | bytes 258056 | tf_op jit(solution)/shard_map/ppermute | solution.py:14
  66.9 0.0 copy-start.2
  66.9 1.9 collective-permute-start.3
  68.8 0.2 constant_dynamic-update-slice_fusion
  69.0 0.0 collective-permute-done.2
  69.0 5.4 %collective-permute-done.3 = bf16[3,14,1024]{2,1,0:T(8,128)(2,1)S(1)} collective-permute-done((bf16[3,14,1024]{2,1,0:T(8,128)(2,1)S(1)}, bf16[3,14,1024]{2,1,0:T(8,128)(2,1)S(1)}, u32[]{:S(2)}, u32[]{:S(2)}) %collective-permute-start.3) | collective-permute-done | bytes 86048 | tf_op jit(solution)/shard_map/ppermute | solution.py:17
  74.4 0.6 maximum_maximum_fusion
  75.0 0.0 copy-done.2
  75.0 0.0 copy-start.3
  75.1 0.0 copy-start.4
  75.1 9.4 %fusion.77 = (f32[32,8]{1,0:T(8,128)S(1)}, f32[32,8,1024]{2,1,0:T(8,128)S(1)}) fusion(f32[1024]{0:T(1024)S(1)} %bitcast.125, bf16[35,14,1024]{2,1,0:T(8,128)(2,1)S(1)} %get-tuple-element.8, f32[1024]{0:T(1024)S(1)} %bitcast.124, f32[1024]{0:T(1024)S(1)} %bitcast.123, f32[1024]{0:T(1024)S(1)} %bitcast.122, f32[1024]{0:T(1024)S(1)} %bitcast.121, ...), kind=kLoop, calls=%fused_computation.101 | loop fusion | flops 41156352 | bytes 25568256 | tf_op jit(solution)/shard_map/reduce_sum | solution.py:60
  84.5 0.3 multiply_reduce_fusion
  84.8 0.0 copy-done.3
  84.8 0.0 copy-done.4
  84.8 1.0 fusion.44
  85.8 0.0 all-gather.10.cloned.1.call-update
  85.9 0.2 reduce-scatter.2.cloned.1.call-start
  86.1 7.4 %all-gather.12.cloned.1.call-done = bf16[64,2,8,1024]{3,2,1,0:T(8,128)(2,1)} async-done(((bf16[4,2,8,1024]{3,2,1,0:T(8,128)(2,1)}), bf16[64,2,8,1024]{3,2,1,0:T(8,128)(2,1)}) %all-gather.12.cloned.1.call-update) | async-done | bytes 2097168 | tf_op jit(solution)/shard_map/all_gather | solution.py:32
  93.5 1.8 copy.13
  95.3 70.2 %all-gather.14.cloned.1.call-done = bf16[64,2,8,1024]{3,2,1,0:T(8,128)(2,1)} async-done(((bf16[4,2,8,1024]{3,2,1,0:T(8,128)(2,1)}), bf16[64,2,8,1024]{3,2,1,0:T(8,128)(2,1)}) %all-gather.14.cloned.1.call-update) | async-done | bytes 2097168 | tf_op jit(solution)/shard_map/all_gather | solution.py:32
  165.5 0.0 copy-start.7
  165.5 3.3 %copy.14 = bf16[4,16,2,8,1024]{4,3,2,1,0:T(8,128)(2,1)} copy(bf16[4,16,2,8,1024]{4,3,2,0,1:T(8,128)(2,1)} %bitcast.70) | data formatting | bytes 4194304 | tf_op jit(solution)/shard_map/transpose | solution.py:33
  168.8 39.6 %all-gather.10.cloned.1.call-done = bf16[1024,1024]{1,0:T(8,128)(2,1)} async-done(((bf16[256,1024]{1,0:T(8,128)(2,1)}), bf16[1024,1024]{1,0:T(8,128)(2,1)}) %all-gather.10.cloned.1.call-update) | async-done | bytes 2097168 | tf_op jit(solution)/shard_map/all_gather | solution.py:66
  208.4 0.0 copy-done.7
  208.4 15.5 %fusion.14 = bf16[1024,1024]{1,0:T(8,128)(2,1)} fusion(bf16[1024,1024]{1,0:T(8,128)(2,1)} %bitcast.72, f32[1024]{0:T(1024)S(1)} %copy-done.7, bf16[1024,1024]{1,0:T(8,128)(2,1)} %all-gather.10.cloned.1.call-done, bf16[1024,1024]{1,0:T(8,128)(2,1)S(1)} %bitcast.71), kind=kOutput, calls=%fused_computation.21 | convolution fusion | flops 4365221888 | bytes 8392704 | tf_op jit(solution)/shard_map/dot_general | solution.py:69
  223.9 0.0 copy-start.5
  223.9 0.0 copy-start.6
  223.9 0.0 reduce-scatter.2.cloned.1.call-update
  224.0 53.0 %reduce-scatter.2.cloned.1.call-done = bf16[256,1024]{1,0:T(8,128)(2,1)} async-done(((bf16[1024,1024]{1,0:T(8,128)(2,1)}), bf16[256,1024]{1,0:T(8,128)(2,1)}) %reduce-scatter.2.cloned.1.call-update) | async-done | bytes 524304 | tf_op jit(solution)/shard_map/reduce_scatter | solution.py:75
  277.0 0.0 copy-done.5
  277.0 0.0 copy-done.6
  277.0 2.0 fusion.42
  (4 shorter events, 0.1 us)
Async XLA Ops:
  6.5 47.2 %copy-start = (bf16[32,8,1024]{2,1,0:T(8,128)(2,1)S(1)}, bf16[32,8,1024]{2,1,0:T(8,128)(2,1)}, u32[]{:S(2)}) copy-start(bf16[32,8,1024]{2,1,0:T(8,128)(2,1)} %param.10) | copy-start | bytes 1572868
  6.5 47.2 %copy-start.1 = (bf16[7,7,1024]{2,1,0:T(8,128)(2,1)S(1)}, bf16[7,7,1024]{2,1,0:T(8,128)(2,1)}, u32[]{:S(2)}) copy-start(bf16[7,7,1024]{2,1,0:T(8,128)(2,1)} %param.11) | copy-start | bytes 301060
  6.5 87.0 %all-gather.12.cloned.1.call-start = ((), (), s32[]{:S(2)}) async-start(), calls=%async_computation.3 | async-start | bytes 2228224 | tf_op jit(solution)/shard_map/all_gather | solution.py:32
  21.2 144.3 %all-gather.14.cloned.1.call-start = ((), (), s32[]{:S(2)}) async-start(), calls=%async_computation.4 | async-start | bytes 2228224 | tf_op jit(solution)/shard_map/all_gather | solution.py:32
  22.7 31.2 %collective-permute-start = (bf16[32,3,1024]{2,1,0:T(4,128)(2,1)S(1)}, bf16[32,3,1024]{2,1,0:T(4,128)(2,1)S(1)}, u32[]{:S(2)}, u32[]{:S(2)}) collective-permute-start(bf16[32,3,1024]{2,1,0:T(4,128)(2,1)S(1)} %get-tuple-element.11), channel_id=1, source_target_pairs={{0,1},{1,2},{2,3},{3,4},{4,5},{5,6},{6,7},{7,8},{8,9},{9,10},{10,1... | collective-permute-start | bytes 589832 | tf_op jit(solution)/shard_map/ppermute | solution.py:14
  25.9 28.0 %collective-permute-start.1 = (bf16[32,3,1024]{2,1,0:T(4,128)(2,1)S(1)}, bf16[32,3,1024]{2,1,0:T(4,128)(2,1)S(1)}, u32[]{:S(2)}, u32[]{:S(2)}) collective-permute-start(bf16[32,3,1024]{2,1,0:T(4,128)(2,1)S(1)} %get-tuple-element.12), channel_id=1, source_target_pairs={{1,0},{2,1},{3,2},{4,3},{5,4},{6,5},{7,6},{8,7},{9,8},{10,9},{11,1... | collective-permute-start | bytes 589832 | tf_op jit(solution)/shard_map/ppermute | solution.py:17
  52.5 155.9 %all-gather.10.cloned.1.call-start = ((), (), s32[]{:S(2)}) async-start(), calls=%async_computation.1 | async-start | bytes 2621440 | tf_op jit(solution)/shard_map/all_gather | solution.py:66
  54.0 15.0 %collective-permute-start.2 = (bf16[3,14,1024]{2,1,0:T(8,128)(2,1)S(1)}, bf16[3,14,1024]{2,1,0:T(8,128)(2,1)S(1)}, u32[]{:S(2)}, u32[]{:S(2)}) collective-permute-start(bf16[3,14,1024]{2,1,0:T(8,128)(2,1)S(1)} %get-tuple-element.9), channel_id=1, source_target_pairs={{0,128},{128,256},{256,384},{1,129},{129,257},{257,385},{2,130},{1... | collective-permute-start | bytes 258056 | tf_op jit(solution)/shard_map/ppermute | solution.py:14
  66.9 8.2 %copy-start.2 = (f32[1024]{0:T(1024)S(1)}, f32[1024]{0:T(1024)}, u32[]{:S(2)}) copy-start(f32[1024]{0:T(1024)} %param.12) | copy-start | bytes 12292
  66.9 7.5 %collective-permute-start.3 = (bf16[3,14,1024]{2,1,0:T(8,128)(2,1)S(1)}, bf16[3,14,1024]{2,1,0:T(8,128)(2,1)S(1)}, u32[]{:S(2)}, u32[]{:S(2)}) collective-permute-start(bf16[3,14,1024]{2,1,0:T(8,128)(2,1)S(1)} %get-tuple-element.10), channel_id=1, source_target_pairs={{128,0},{256,128},{384,256},{129,1},{257,129},{385,257},{130,2},{2... | collective-permute-start | bytes 258056 | tf_op jit(solution)/shard_map/ppermute | solution.py:17
  75.0 9.7 %copy-start.3 = (f32[1024]{0:T(1024)S(1)}, f32[1024]{0:T(1024)}, u32[]{:S(2)}) copy-start(f32[1024]{0:T(1024)} %param.14) | copy-start | bytes 12292
  75.1 9.7 %copy-start.4 = (f32[1024]{0:T(1024)S(1)}, f32[1024]{0:T(1024)}, u32[]{:S(2)}) copy-start(f32[1024]{0:T(1024)} %param.13) | copy-start | bytes 12292
  85.9 191.1 %reduce-scatter.2.cloned.1.call-start = ((), (), s32[]{:S(2)}) async-start(), calls=%async_computation.2 | async-start | bytes 2621440 | tf_op jit(solution)/shard_map/reduce_scatter | solution.py:75
  165.5 42.9 %copy-start.7 = (f32[1024]{0:T(1024)S(1)}, f32[1024]{0:T(1024)}, u32[]{:S(2)}) copy-start(f32[1024]{0:T(1024)} %param.16) | copy-start | bytes 12292
  223.9 53.1 %copy-start.5 = (f32[1024]{0:T(1024)S(1)}, f32[1024]{0:T(1024)}, u32[]{:S(2)}) copy-start(f32[1024]{0:T(1024)} %param.18) | copy-start | bytes 12292
  223.9 53.1 %copy-start.6 = (f32[1024]{0:T(1024)S(1)}, f32[1024]{0:T(1024)}, u32[]{:S(2)}) copy-start(f32[1024]{0:T(1024)} %param.19) | copy-start | bytes 12292
Sparse Core Ops, SparseCore 0:
  21.3 72.1 all-gather.11
  95.6 69.8 all-gather.13
  167.6 40.7 all-gather.9
  224.1 52.8 reduce-scatter.1
where the time goes:
time: 286 us
  waiting for transfers between devices  176 us (62%)
  starting transfers between devices  31 us (11%)
  blocking collectives  28.5 us (10%)
  matrix products  15.5 us (5%)
  other arithmetic  13.5 us (5%)
  between operations  13.3 us (5%)
  local copies, waits for them, and re-layouts  7.98 us (3%)
    all_gather x2, waiting for transfers between devices, staged_gather(): part = lax.all_gather(part, 'lon', axis=0, axis_index_groups=by_z)  77.6 us
    reduce_scatter x1, waiting for transfers between devices, local(): lax.psum_scatter(partial_out.astype(jnp.bfloat16), 'lat', scatter_dimensi...  53 us
    all_gather x1, waiting for transfers between devices, local(): gathered = lax.all_gather(normed, 'lat', axis=0, tiled=True)  39.6 us
    all_gather x2, blocking collectives, staged_gather(): part = lax.all_gather(part, 'lon', axis=0, axis_index_groups=by_x)  20.1 us
    ppermute x2, starting transfers between devices, with_halo(): lax.ppermute(lax.slice_in_dim(block, block.shape[dim] - width, None, axis...  16.1 us
    dot_general x1, matrix products, local(): lax.dot_general(hidden, staged_gather(down_weight), (((1,), (1,)), ((), (...  15.5 us
    ppermute x2, starting transfers between devices, with_halo(): lax.ppermute(lax.slice_in_dim(block, 0, width, axis=dim), axis, backward)  14.6 us
    reduce_sum x1, other arithmetic, local(): centre = jnp.mean(total, axis=-1, keepdims=True)  9.42 us
  transfers between devices with their start and end apart: 8, of which 5 were waited for; matrix products, arithmetic and copies ran while one was open for 7% of the time, Pallas kernels for 0%

commit v1 on v0

--- a/solution.py
+++ b/solution.py
@@ -63,7 +63,9 @@
         jnp.bfloat16
     )
     normed = normed.reshape(row_count * col_count, chan_count)
-    gathered = lax.all_gather(normed, "lat", axis=0, tiled=True)
+    gathered = jnp.concatenate(
+        lax.all_to_all(jnp.stack([normed] * lax.axis_size("lat")), "lat", 0, 0), axis=0
+    )
     pre = jnp.dot(gathered, staged_gather(up_weight), preferred_element_type=jnp.float32) + up_bias
     hidden = jax.nn.gelu(pre, approximate=False).astype(jnp.bfloat16)
     partial_out = lax.dot_general(

time: 286 us -> 254 us (0.89)
  waiting for transfers between devices: 176 us -> 135 us
  local copies, waits for them, and re-layouts: 7.98 us -> 13.3 us
  starting transfers between devices: 31 us -> 34.6 us
    all_gather x1 -> x0, waiting for transfers between devices: 39.6 us -> none  [local(): gathered = lax.all_gather(normed, 'lat', axis=0, tiled=True)]
    all_gather x2, waiting for transfers between devices: 77.6 us -> 69.5 us  [staged_gather(): part = lax.all_gather(part, 'lon', axis=0, axis_index_groups=by_z)]
    reduce_scatter x1, waiting for transfers between devices: 53 us -> 60 us  [local(): lax.psum_scatter(partial_out.astype(jnp.bfloat16), 'lat', scatter_dimensi...]
    all_to_all x0 -> x1, starting transfers between devices: none -> 3.6 us  [local(): lax.all_to_all(jnp.stack([normed] * lax.axis_size('lat')), 'lat', 0, 0)]
  transfers between devices with their start and end apart: 8 -> 8, of which waited for: 5 -> 4; matrix products, arithmetic and copies ran while one was open for 7% -> 9% of each run, Pallas kernels for 0% -> 0%
where the time goes in v1:
time: 254 us; the launch traced here: 253 us
  waiting for transfers between devices  135 us (53%)
  starting transfers between devices  34.6 us (14%)
  blocking collectives  28.5 us (11%)
  matrix products  16 us (6%)
  local copies, waits for them, and re-layouts  13.3 us (5%)
  between operations  13.3 us (5%)
  other arithmetic  12.7 us (5%)
    all_gather x2, waiting for transfers between devices, staged_gather(): part = lax.all_gather(part, 'lon', axis=0, axis_index_groups=by_z)  69.5 us
    reduce_scatter x1, waiting for transfers between devices, local(): lax.psum_scatter(partial_out.astype(jnp.bfloat16), 'lat', scatter_dimensi...  60 us
    all_gather x2, blocking collectives, staged_gather(): part = lax.all_gather(part, 'lon', axis=0, axis_index_groups=by_x)  20.1 us
    ppermute x2, starting transfers between devices, with_halo(): lax.ppermute(lax.slice_in_dim(block, block.shape[dim] - width, None, axis...  16.1 us
    dot_general x1, matrix products, local(): lax.dot_general(hidden, staged_gather(down_weight), (((1,), (1,)), ((), (...  16 us
    ppermute x2, starting transfers between devices, with_halo(): lax.ppermute(lax.slice_in_dim(block, 0, width, axis=dim), axis, backward)  14.6 us
    reduce_sum x1, other arithmetic, local(): centre = jnp.mean(total, axis=-1, keepdims=True)  9.42 us
    all_gather x2, blocking collectives, staged_gather(): part = lax.all_gather(shard, 'lon', axis=0, axis_index_groups=by_y)  8.31 us
  transfers between devices with their start and end apart: 8, of which 4 were waited for; matrix products, arithmetic and copies ran while one was open for 9% of the time, Pallas kernels for 0%

profile of v1, /device:TPU:1, one launch (start us, length us, event | category | flops | bytes accessed | tf_op | source)
XLA Modules:
  0.0 253.3 jit_solution(7434141498309080351)
XLA Ops:
  6.5 0.0 copy-start
  6.5 0.0 all-gather.9.cloned.1.call-start
  6.5 4.3 %all-gather = bf16[16,1024]{1,0:T(8,128)(2,1)S(1)} all-gather(bf16[8,1024]{1,0:T(8,128)(2,1)} %param.15), channel_id=2, replica_groups={{0,1},{2,3},{4,5},{6,7},{8,9},{10,11},{12,13},{14,15},{16,17},{18,19},{..., dimensions={0}, use_global_device_ids=true | all-gather | bytes 49152 | tf_op jit(solution)/shard_map/all_gather | solution.py:30
  10.8 10.3 %all-gather.1 = bf16[8,8,1024]{2,1,0:T(8,128)(2,1)} all-gather(bf16[2,8,1024]{2,1,0:T(8,128)(2,1)S(1)} %bitcast.77), channel_id=3, replica_groups={{0,32,64,96},{1,33,65,97},{2,34,66,98},{3,35,67,99},{4,36,68,100},{5,37..., dimensions={0}, use_global_device_ids=true | all-gather | bytes 163840 | tf_op jit(solution)/shard_map/all_gather | solution.py:31
  21.1 0.0 all-gather.9.cloned.1.call-update
  21.2 0.0 all-gather.11.cloned.1.call-start
  21.2 1.4 fusion.79
  22.6 3.2 %collective-permute-start = (bf16[32,3,1024]{2,1,0:T(4,128)(2,1)S(1)}, bf16[32,3,1024]{2,1,0:T(4,128)(2,1)S(1)}, u32[]{:S(2)}, u32[]{:S(2)}) collective-permute-start(bf16[32,3,1024]{2,1,0:T(4,128)(2,1)S(1)} %get-tuple-element.11), channel_id=1, source_target_pairs={{0,1},{1,2},{2,3},{3,4},{4,5},{5,6},{6,7},{7,8},{8,9},{9,10},{10,1... | collective-permute-start | bytes 589832 | tf_op jit(solution)/shard_map/ppermute | solution.py:14
  25.9 12.7 %collective-permute-start.1 = (bf16[32,3,1024]{2,1,0:T(4,128)(2,1)S(1)}, bf16[32,3,1024]{2,1,0:T(4,128)(2,1)S(1)}, u32[]{:S(2)}, u32[]{:S(2)}) collective-permute-start(bf16[32,3,1024]{2,1,0:T(4,128)(2,1)S(1)} %get-tuple-element.12), channel_id=1, source_target_pairs={{1,0},{2,1},{3,2},{4,3},{5,4},{6,5},{7,6},{8,7},{9,8},{10,9},{11,1... | collective-permute-start | bytes 589832 | tf_op jit(solution)/shard_map/ppermute | solution.py:17
  38.6 4.0 %all-gather.3 = bf16[16,1024]{1,0:T(8,128)(2,1)S(1)} all-gather(bf16[8,1024]{1,0:T(8,128)(2,1)} %param.17), channel_id=5, replica_groups={{0,1},{2,3},{4,5},{6,7},{8,9},{10,11},{12,13},{14,15},{16,17},{18,19},{..., dimensions={0}, use_global_device_ids=true | all-gather | bytes 49152 | tf_op jit(solution)/shard_map/all_gather | solution.py:30
  42.6 9.8 %all-gather.4 = bf16[8,8,1024]{2,1,0:T(8,128)(2,1)} all-gather(bf16[2,8,1024]{2,1,0:T(8,128)(2,1)S(1)} %bitcast.78), channel_id=6, replica_groups={{0,32,64,96},{1,33,65,97},{2,34,66,98},{3,35,67,99},{4,36,68,100},{5,37..., dimensions={0}, use_global_device_ids=true | all-gather | bytes 163840 | tf_op jit(solution)/shard_map/all_gather | solution.py:31
  52.4 0.0 all-gather.11.cloned.1.call-update
  52.5 1.2 fusion.80
  53.6 1.2 fusion.81
  54.9 0.0 copy-done
  54.9 1.1 fusion.82
  56.0 0.0 collective-permute-done
  56.0 0.0 collective-permute-done.1
  56.0 0.1 pad_maximum_fusion.4
  56.1 12.9 %collective-permute-start.2 = (bf16[3,14,1024]{2,1,0:T(8,128)(2,1)S(1)}, bf16[3,14,1024]{2,1,0:T(8,128)(2,1)S(1)}, u32[]{:S(2)}, u32[]{:S(2)}) collective-permute-start(bf16[3,14,1024]{2,1,0:T(8,128)(2,1)S(1)} %get-tuple-element.9), channel_id=1, source_target_pairs={{0,128},{128,256},{256,384},{1,129},{129,257},{257,385},{2,130},{1... | collective-permute-start | bytes 258056 | tf_op jit(solution)/shard_map/ppermute | solution.py:14
  69.0 0.0 copy-start.1
  69.0 1.9 collective-permute-start.3
  71.0 0.2 constant_dynamic-update-slice_fusion
  71.1 0.0 collective-permute-done.2
  71.2 5.3 %collective-permute-done.3 = bf16[3,14,1024]{2,1,0:T(8,128)(2,1)S(1)} collective-permute-done((bf16[3,14,1024]{2,1,0:T(8,128)(2,1)S(1)}, bf16[3,14,1024]{2,1,0:T(8,128)(2,1)S(1)}, u32[]{:S(2)}, u32[]{:S(2)}) %collective-permute-start.3) | collective-permute-done | bytes 86048 | tf_op jit(solution)/shard_map/ppermute | solution.py:17
  76.5 0.6 maximum_maximum_fusion
  77.1 0.0 copy-done.1
  77.1 0.0 copy-start.2
  77.1 0.0 copy-start.3
  77.2 9.4 %fusion.77 = (f32[32,8]{1,0:T(8,128)S(1)}, f32[32,8,1024]{2,1,0:T(8,128)S(1)}) fusion(f32[1024]{0:T(1024)S(1)} %bitcast.127, bf16[35,14,1024]{2,1,0:T(8,128)(2,1)S(1)} %get-tuple-element.8, f32[1024]{0:T(1024)S(1)} %bitcast.126, f32[1024]{0:T(1024)S(1)} %bitcast.125, f32[1024]{0:T(1024)S(1)} %bitcast.124, f32[1024]{0:T(1024)S(1)} %bitcast.123, ...), kind=kLoop, calls=%fused_computation.101 | loop fusion | flops 41156352 | bytes 25568256 | tf_op jit(solution)/shard_map/reduce_sum | solution.py:60
  86.6 0.3 multiply_reduce_fusion
  86.8 0.0 copy-done.2
  86.9 0.0 copy-done.3
  86.9 0.2 fusion.44
  87.1 1.6 stack.3
  88.7 3.6 %all-to-all-start = ((bf16[4,256,1024]{2,1,0:T(8,128)(2,1)}), bf16[4,256,1024]{2,1,0:T(8,128)(2,1)S(1)}, u32[]{:S(2)}, u32[]{:S(2)}) async-start(bf16[4,256,1024]{2,1,0:T(8,128)(2,1)} %stack.3), calls=%async_computation | async-start | bytes 4194304 | tf_op jit(solution)/shard_map/all_to_all | solution.py:67
  92.3 0.2 reduce-scatter.2.cloned.1.call-start
  92.6 1.0 all-gather.9.cloned.1.call-done
  93.5 3.3 %copy.13 = bf16[4,16,2,8,1024]{4,3,2,1,0:T(8,128)(2,1)} copy(bf16[4,16,2,8,1024]{4,3,2,0,1:T(8,128)(2,1)} %bitcast.70) | data formatting | bytes 4194304 | tf_op jit(solution)/shard_map/transpose | solution.py:33
  96.8 68.6 %all-gather.11.cloned.1.call-done = bf16[64,2,8,1024]{3,2,1,0:T(8,128)(2,1)} async-done(((bf16[4,2,8,1024]{3,2,1,0:T(8,128)(2,1)}), bf16[64,2,8,1024]{3,2,1,0:T(8,128)(2,1)}) %all-gather.11.cloned.1.call-update) | async-done | bytes 2097168 | tf_op jit(solution)/shard_map/all_gather | solution.py:32
  165.4 0.0 copy-start.6
  165.4 3.3 %copy.14 = bf16[4,16,2,8,1024]{4,3,2,1,0:T(8,128)(2,1)} copy(bf16[4,16,2,8,1024]{4,3,2,0,1:T(8,128)(2,1)} %bitcast.71) | data formatting | bytes 4194304 | tf_op jit(solution)/shard_map/transpose | solution.py:33
  168.6 0.0 all-to-all-done
  168.6 0.0 copy-done.6
  168.6 16.0 %fusion.14 = bf16[1024,1024]{1,0:T(8,128)(2,1)} fusion(bf16[1024,1024]{1,0:T(8,128)(2,1)} %bitcast.74, f32[1024]{0:T(1024)S(1)} %copy-done.6, bf16[1024,1024]{1,0:T(8,128)(2,1)S(1)} %bitcast.72, bf16[1024,1024]{1,0:T(8,128)(2,1)} %bitcast.73), kind=kOutput, calls=%fused_computation.21 | convolution fusion | flops 4365221888 | bytes 8392704 | tf_op jit(solution)/shard_map/dot_general | solution.py:71
  184.7 0.0 copy-start.4
  184.7 0.0 copy-start.5
  184.7 0.0 reduce-scatter.2.cloned.1.call-update
  184.7 60.0 %reduce-scatter.2.cloned.1.call-done = bf16[256,1024]{1,0:T(8,128)(2,1)} async-done(((bf16[1024,1024]{1,0:T(8,128)(2,1)}), bf16[256,1024]{1,0:T(8,128)(2,1)}) %reduce-scatter.2.cloned.1.call-update) | async-done | bytes 524304 | tf_op jit(solution)/shard_map/reduce_scatter | solution.py:77
  244.7 0.0 copy-done.4
  244.7 0.0 copy-done.5
  244.7 2.0 fusion.42
  (3 shorter events, 0.1 us)
Async XLA Ops:
  6.5 48.3 %copy-start = (bf16[32,8,1024]{2,1,0:T(8,128)(2,1)S(1)}, bf16[32,8,1024]{2,1,0:T(8,128)(2,1)}, u32[]{:S(2)}) copy-start(bf16[32,8,1024]{2,1,0:T(8,128)(2,1)} %param.10) | copy-start | bytes 1572868
  6.5 87.0 %all-gather.9.cloned.1.call-start = ((), (), s32[]{:S(2)}) async-start(), calls=%async_computation.3 | async-start | bytes 2228224 | tf_op jit(solution)/shard_map/all_gather | solution.py:32
  21.2 144.2 %all-gather.11.cloned.1.call-start = ((), (), s32[]{:S(2)}) async-start(), calls=%async_computation.4 | async-start | bytes 2228224 | tf_op jit(solution)/shard_map/all_gather | solution.py:32
  22.6 33.3 %collective-permute-start = (bf16[32,3,1024]{2,1,0:T(4,128)(2,1)S(1)}, bf16[32,3,1024]{2,1,0:T(4,128)(2,1)S(1)}, u32[]{:S(2)}, u32[]{:S(2)}) collective-permute-start(bf16[32,3,1024]{2,1,0:T(4,128)(2,1)S(1)} %get-tuple-element.11), channel_id=1, source_target_pairs={{0,1},{1,2},{2,3},{3,4},{4,5},{5,6},{6,7},{7,8},{8,9},{9,10},{10,1... | collective-permute-start | bytes 589832 | tf_op jit(solution)/shard_map/ppermute | solution.py:14
  25.9 30.1 %collective-permute-start.1 = (bf16[32,3,1024]{2,1,0:T(4,128)(2,1)S(1)}, bf16[32,3,1024]{2,1,0:T(4,128)(2,1)S(1)}, u32[]{:S(2)}, u32[]{:S(2)}) collective-permute-start(bf16[32,3,1024]{2,1,0:T(4,128)(2,1)S(1)} %get-tuple-element.12), channel_id=1, source_target_pairs={{1,0},{2,1},{3,2},{4,3},{5,4},{6,5},{7,6},{8,7},{9,8},{10,9},{11,1... | collective-permute-start | bytes 589832 | tf_op jit(solution)/shard_map/ppermute | solution.py:17
  56.1 15.0 %collective-permute-start.2 = (bf16[3,14,1024]{2,1,0:T(8,128)(2,1)S(1)}, bf16[3,14,1024]{2,1,0:T(8,128)(2,1)S(1)}, u32[]{:S(2)}, u32[]{:S(2)}) collective-permute-start(bf16[3,14,1024]{2,1,0:T(8,128)(2,1)S(1)} %get-tuple-element.9), channel_id=1, source_target_pairs={{0,128},{128,256},{256,384},{1,129},{129,257},{257,385},{2,130},{1... | collective-permute-start | bytes 258056 | tf_op jit(solution)/shard_map/ppermute | solution.py:14
  69.0 8.1 %copy-start.1 = (f32[1024]{0:T(1024)S(1)}, f32[1024]{0:T(1024)}, u32[]{:S(2)}) copy-start(f32[1024]{0:T(1024)} %param.12) | copy-start | bytes 12292
  69.0 7.4 %collective-permute-start.3 = (bf16[3,14,1024]{2,1,0:T(8,128)(2,1)S(1)}, bf16[3,14,1024]{2,1,0:T(8,128)(2,1)S(1)}, u32[]{:S(2)}, u32[]{:S(2)}) collective-permute-start(bf16[3,14,1024]{2,1,0:T(8,128)(2,1)S(1)} %get-tuple-element.10), channel_id=1, source_target_pairs={{128,0},{256,128},{384,256},{129,1},{257,129},{385,257},{130,2},{2... | collective-permute-start | bytes 258056 | tf_op jit(solution)/shard_map/ppermute | solution.py:17
  77.1 9.7 %copy-start.2 = (f32[1024]{0:T(1024)S(1)}, f32[1024]{0:T(1024)}, u32[]{:S(2)}) copy-start(f32[1024]{0:T(1024)} %param.14) | copy-start | bytes 12292
  77.1 9.7 %copy-start.3 = (f32[1024]{0:T(1024)S(1)}, f32[1024]{0:T(1024)}, u32[]{:S(2)}) copy-start(f32[1024]{0:T(1024)} %param.13) | copy-start | bytes 12292
  88.7 79.9 %all-to-all-start = ((bf16[4,256,1024]{2,1,0:T(8,128)(2,1)}), bf16[4,256,1024]{2,1,0:T(8,128)(2,1)S(1)}, u32[]{:S(2)}, u32[]{:S(2)}) async-start(bf16[4,256,1024]{2,1,0:T(8,128)(2,1)} %stack.3), calls=%async_computation | async-start | bytes 4194304 | tf_op jit(solution)/shard_map/all_to_all | solution.py:67
  92.3 152.3 %reduce-scatter.2.cloned.1.call-start = ((), (), s32[]{:S(2)}) async-start(), calls=%async_computation.2 | async-start | bytes 2621440 | tf_op jit(solution)/shard_map/reduce_scatter | solution.py:77
  165.4 3.3 %copy-start.6 = (f32[1024]{0:T(1024)S(1)}, f32[1024]{0:T(1024)}, u32[]{:S(2)}) copy-start(f32[1024]{0:T(1024)} %param.16) | copy-start | bytes 12292
  184.7 60.0 %copy-start.4 = (f32[1024]{0:T(1024)S(1)}, f32[1024]{0:T(1024)}, u32[]{:S(2)}) copy-start(f32[1024]{0:T(1024)} %param.18) | copy-start | bytes 12292
  184.7 60.0 %copy-start.5 = (f32[1024]{0:T(1024)S(1)}, f32[1024]{0:T(1024)}, u32[]{:S(2)}) copy-start(f32[1024]{0:T(1024)} %param.19) | copy-start | bytes 12292
Sparse Core Ops, SparseCore 0:
  21.3 72.1 all-gather.8
  95.6 69.7 all-gather.10
  184.8 59.8 reduce-scatter.1
